TPU v7x, 512 devices: a whole 4x8x8 slice. The times are simulated.
512 devices in a mesh: ab: 32 (over z, x), cd: 16 (over y, core).
Axes of the slice: x: 4, y: 8, z: 8, core: 2. Of those that a mesh axis runs over, the one named last changes fastest.
Arguments:
- amplitudes: float32 [512, 8192], P('ab', 'cd'), may hold values from -6 to 6
- integrals: float32 [65536, 8192], P('ab', 'cd'), may hold values from -0.125 to 0.125
- ij_pairs: int32 [512, 2], P('cd'), may hold values from 0 to 127
- ab_pairs: int32 [65536, 2], P('ab'), may hold values from 0 to 1535
- eps_occ: float32 [128], replicated, may hold values from -1.5 to -0.3
- eps_vir: float32 [1536], replicated, may hold values from 0.1 to 2.5
Outputs:
- ladder: float32 [512, 65536], P('cd', 'ab')
- update: float32 [512, 65536], P('cd', 'ab')
All inputs are finite; a program needn't handle non-finite values.
Results may differ from a plain program's by a relative error of at most 0.00015.
Values sent between devices are 32-bit elements; how exact they have to be, the bound alone decides.
A program may use at most 64 MiB of HBM per device.

v0:
```python
import jax
import jax.numpy as jnp
from jax import lax
from jax.sharding import PartitionSpec as P


def lookup_energy(indices, energies):
    positions = lax.broadcasted_iota(jnp.int32, (indices.shape[0], energies.shape[0]), 1)
    picked = jnp.where(indices[:, None] == positions, energies[None, :], jnp.float32(0.0))
    return jnp.sum(picked, axis=1)


def contract_rows(row_block, col_block):
    return lax.dot_general(
        row_block,
        col_block,
        (((1,), (1,)), ((), ())),
        precision=lax.Precision.HIGHEST,
        preferred_element_type=jnp.float32,
    )


def on_device(amplitudes, integrals, ij_pairs, ab_pairs, eps_occ, eps_vir):
    partial_value = contract_rows(lax.all_gather(amplitudes, "ab", axis=0, tiled=True), integrals)
    ladder = lax.psum_scatter(partial_value, "cd", scatter_dimension=0, tiled=True)
    first_occ = lookup_energy(ij_pairs[:, 0], eps_occ)[:, None]
    second_occ = lookup_energy(ij_pairs[:, 1], eps_occ)[:, None]
    first_vir = lookup_energy(ab_pairs[:, 0], eps_vir)[None, :]
    second_vir = lookup_energy(ab_pairs[:, 1], eps_vir)[None, :]
    denominator = first_occ + second_occ - first_vir - second_vir
    update = ladder / denominator
    return (ladder, update)


def solution(mesh):
    in_specs = (P("ab", "cd"), P("ab", "cd"), P("cd", None), P("ab", None), P(), P())
    out_specs = (P("cd", "ab"), P("cd", "ab"))
    return jax.shard_map(
        on_device, mesh=mesh, in_specs=in_specs, out_specs=out_specs, check_vma=False
    )
```

profile of v0, /device:TPU:27, one launch (start us, length us, event | category | flops | bytes accessed | tf_op | source)
XLA Modules:
  0.0 179.7 jit_solution(8097404686899207612)
XLA Ops:
  7.2 0.0 all-gather.2.cloned.1.call-start
  7.2 0.7 all-gather.2.cloned.1.call-update
  7.9 0.0 reduce-scatter.2.cloned.1.call-start
  7.9 84.6 %all-gather.2.cloned.1.call-done = f32[512,512]{1,0:T(8,128)} async-done(((f32[16,512]{1,0:T(8,128)}), f32[512,512]{1,0:T(8,128)}) %all-gather.2.cloned.1.call-update) | async-done | bytes 1048592 | tf_op jit(solution)/shard_map/all_gather | solution.py:24
  92.5 10.4 %fusion.1 = f32[512,2048]{1,0:T(8,128)} fusion(f32[512,512]{1,0:T(8,128)} %all-gather.2.cloned.1.call-done, f32[2048,512]{1,0:T(8,128)} %param.7), kind=kOutput, calls=%fused_computation.12 | convolution fusion | flops 6442450944 | bytes 9437184 | tf_op jit(solution)/shard_map/dot_general | solution.py:14
  102.9 0.0 copy-start.1
  102.9 0.0 copy-start.2
  102.9 0.0 copy-start
  102.9 0.0 copy-start.3
  102.9 0.0 reduce-scatter.2.cloned.1.call-update
  102.9 0.6 copy-done.1
  103.5 0.0 copy-done.2
  103.5 0.2 select_reduce_fusion.2
  103.7 0.0 copy-done
  103.8 0.0 copy-done.3
  103.8 3.9 %select_reduce_fusion.1 = (f32[2048]{0:T(1024)S(1)}, f32[2048]{0:T(1024)S(1)}) fusion(f32[1536]{0:T(1024)S(1)} %copy-done.3, s32[2048]{0:T(1024)S(1)} %bitcast.9, s32[2048]{0:T(1024)S(1)} %bitcast.8), kind=kLoop, calls=%fused_computation.2 | loop fusion | flops 18870272 | bytes 38912 | tf_op jit(solution)/shard_map/reduce_sum | solution.py:10
  107.7 63.4 %reduce-scatter.2.cloned.1.call-done = f32[32,2048]{1,0:T(8,128)} async-done(((f32[512,2048]{1,0:T(8,128)}), f32[32,2048]{1,0:T(8,128)}) %reduce-scatter.2.cloned.1.call-update) | async-done | bytes 262160 | tf_op jit(solution)/shard_map/reduce_scatter | solution.py:25
  171.1 1.8 subtract_divide_fusion
  (3 shorter events, 0.0 us)
Async XLA Ops:
  7.2 85.3 %all-gather.2.cloned.1.call-start = ((), (), s32[]{:S(2)}) async-start(), calls=%async_computation.1 | async-start | bytes 1081344 | tf_op jit(solution)/shard_map/all_gather | solution.py:24
  7.9 163.2 %reduce-scatter.2.cloned.1.call-start = ((), (), s32[]{:S(2)}) async-start(), calls=%async_computation.2 | async-start | bytes 4456448 | tf_op jit(solution)/shard_map/reduce_scatter | solution.py:25
  102.9 0.7 copy-start.1
  102.9 0.7 copy-start.2
  102.9 0.9 copy-start
  102.9 0.9 copy-start.3
Sparse Core Ops, SparseCore 0:
  11.2 81.2 all-gather.1
  103.0 67.9 reduce-scatter.1
where the time goes:
time: 180 us
  waiting for transfers between devices  149 us (83%)
  between operations  14.1 us (8%)
  matrix products  10.4 us (6%)
  other arithmetic  5.86 us (3%)
    all_gather x1, waiting for transfers between devices, on_device(): lax.all_gather(amplitudes, 'ab', axis=0, tiled=True)  84.6 us
    reduce_scatter x1, waiting for transfers between devices, on_device(): lax.psum_scatter(partial_value, 'cd', scatter_dimension=0, tiled=True)  63.4 us
    dot_general x1, matrix products, contract_rows(): lax.dot_general(row_block, col_block, (((1,), (1,)), ((), ())), precision...  10.4 us
    reduce_sum x2, other arithmetic, lookup_energy(): return jnp.sum(picked, axis=1)  4.09 us
  transfers between devices with their start and end apart: 2, of which 2 were waited for; matrix products, arithmetic and copies ran while one was open for 2% of the time, Pallas kernels for 0%

commit v1 on v0

--- a/solution.py
+++ b/solution.py
@@ -21,7 +21,10 @@
 
 
 def on_device(amplitudes, integrals, ij_pairs, ab_pairs, eps_occ, eps_vir):
-    partial_value = contract_rows(lax.all_gather(amplitudes, "ab", axis=0, tiled=True), integrals)
+    divide_patches = lambda mat: jnp.concatenate(
+        lax.all_to_all(jnp.stack([mat] * lax.axis_size("ab"), 0), "ab", 0, 0), axis=0
+    )
+    partial_value = contract_rows(divide_patches(amplitudes), integrals)
     ladder = lax.psum_scatter(partial_value, "cd", scatter_dimension=0, tiled=True)
     first_occ = lookup_energy(ij_pairs[:, 0], eps_occ)[:, None]
     second_occ = lookup_energy(ij_pairs[:, 1], eps_occ)[:, None]

time: 180 us -> 131 us (0.73)
  the two profiles are of different devices: /device:TPU:27 before, /device:TPU:29 now
where the time goes in v1:
time: 131 us; the launch traced here: 130 us
  waiting for transfers between devices  59 us (45%)
  blocking collectives  39.6 us (30%)
  between operations  14.1 us (11%)
  matrix products  10.1 us (8%)
  other arithmetic  5.86 us (4%)
  local copies, waits for them, and re-layouts  1.54 us (1%)
    reduce_scatter x1, waiting for transfers between devices, on_device(): lax.psum_scatter(partial_value, 'cd', scatter_dimension=0, tiled=True)  58.9 us
    all_to_all x1, blocking collectives, on_device(): lax.all_to_all(jnp.stack([mat] * lax.axis_size('ab'), 0), 'ab', 0, 0)  39.6 us
    dot_general x1, matrix products, contract_rows(): lax.dot_general(row_block, col_block, (((1,), (1,)), ((), ())), precision...  10.1 us
    reduce_sum x2, other arithmetic, lookup_energy(): return jnp.sum(picked, axis=1)  4.09 us
  transfers between devices with their start and end apart: 1, of which 1 were waited for; matrix products, arithmetic and copies ran while one was open for 3% of the time, Pallas kernels for 0%

profile of v1, /device:TPU:29, one launch (start us, length us, event | category | flops | bytes accessed | tf_op | source)
XLA Modules:
  0.0 130.2 jit_solution(6418490993698102634)
XLA Ops:
  7.2 0.0 reduce-scatter.2.cloned.1.call-start
  7.2 0.9 stack.2
  8.1 39.6 %all_to_all.5 = f32[32,16,512]{2,1,0:T(8,128)S(1)} all-to-all(f32[32,16,512]{2,1,0:T(8,128)S(1)} %stack.2), channel_id=1, replica_groups=mesh['ab'=32,'cd'=16] {'ab'}, dimensions={0} | all-to-all | bytes 2097152 | tf_op jit(solution)/shard_map/all_to_all | solution.py:25
  47.7 10.1 %fusion.1 = f32[512,2048]{1,0:T(8,128)} fusion(f32[512,512]{1,0:T(8,128)S(1)} %bitcast.9, f32[2048,512]{1,0:T(8,128)} %param.7), kind=kOutput, calls=%fused_computation.12 | convolution fusion | flops 6442450944 | bytes 9437184 | tf_op jit(solution)/shard_map/dot_general | solution.py:14
  57.8 0.0 copy-start.1
  57.8 0.0 copy-start.2
  57.8 0.0 copy-start
  57.8 0.0 copy-start.3
  57.9 0.0 reduce-scatter.2.cloned.1.call-update
  57.9 0.6 copy-done.1
  58.5 0.0 copy-done.2
  58.5 0.2 select_reduce_fusion.2
  58.7 0.0 copy-done
  58.8 0.0 copy-done.3
  58.8 3.9 %select_reduce_fusion.1 = (f32[2048]{0:T(1024)S(1)}, f32[2048]{0:T(1024)S(1)}) fusion(f32[1536]{0:T(1024)S(1)} %copy-done.3, s32[2048]{0:T(1024)S(1)} %bitcast.11, s32[2048]{0:T(1024)S(1)} %bitcast.10), kind=kLoop, calls=%fused_computation.2 | loop fusion | flops 18870272 | bytes 38912 | tf_op jit(solution)/shard_map/reduce_sum | solution.py:10
  62.7 58.9 %reduce-scatter.2.cloned.1.call-done = f32[32,2048]{1,0:T(8,128)} async-done(((f32[512,2048]{1,0:T(8,128)}), f32[32,2048]{1,0:T(8,128)}) %reduce-scatter.2.cloned.1.call-update) | async-done | bytes 262160 | tf_op jit(solution)/shard_map/reduce_scatter | solution.py:28
  121.6 1.8 %subtract_divide_fusion = f32[32,2048]{1,0:T(8,128)} fusion(f32[32,2048]{1,0:T(8,128)} %reduce-scatter.2.cloned.1.call-done, f32[2048]{0:T(1024)S(1)} %get-tuple-element.3, f32[2048]{0:T(1024)S(1)} %get-tuple-element.2, f32[32]{0:T(128)S(1)} %add.10), kind=kLoop, calls=%fused_computation.4 | loop fusion | flops 196608 | bytes 540800 | tf_op jit(solution)/shard_map/div | solution.py:34
  (3 shorter events, 0.0 us)
Async XLA Ops:
  7.2 114.5 %reduce-scatter.2.cloned.1.call-start = ((), (), s32[]{:S(2)}) async-start(), calls=%async_computation.2 | async-start | bytes 4456448 | tf_op jit(solution)/shard_map/reduce_scatter | solution.py:28
  57.8 0.7 copy-start.1
  57.8 0.7 copy-start.2
  57.8 0.9 copy-start
  57.8 0.9 copy-start.3
Sparse Core Ops, SparseCore 0:
  58.0 63.5 reduce-scatter.1
